TPU v7x, 256 devices: a whole 4x4x8 slice. The times are simulated.
256 devices in a mesh: row: 8 (over y_lo, x), col: 32 (over y_hi, z, core).
Axes of the slice: x: 4, y: 4 (y_hi: 2, y_lo: 2; y = y_hi * 2 + y_lo), z: 8, core: 2. Of those that a mesh axis runs over, the one named last changes fastest.
Arguments:
- volume_plane: bfloat16 [2, 4096, 4096], P(None, 'row', 'col'), may hold values from -4 to 4
- wave_a: bfloat16 [2, 4096, 4096], P(None, 'row', 'col'), may hold values from -4 to 4
- wave_b: bfloat16 [2, 4096, 4096], P(None, 'col', 'row'), may hold values from -4 to 4
- shift_rows: int32 [2, 2, 4096], P(None, None, 'row'), may hold values from -864 to 864, as said below
- fraction_rows: float32 [2, 2, 4096], P(None, None, 'row'), may hold values from -0.5 to 0.5
- shift_columns: int32 [2, 4096], P(None, 'col'), may hold values from -1728 to 1728, as said below
- fraction_columns: float32 [2, 4096], P(None, 'col'), may hold values from -0.5 to 0.5
- travel_distance: float32 [2], replicated, may hold values from 16 to 32
Outputs:
- exit_a: bfloat16 [2, 4096, 4096], P(None, 'row', 'col')
- exit_b: bfloat16 [2, 4096, 4096], P(None, 'col', 'row')
Inputs may be any that keep to these rules, and one draw needn't show every extreme that they name: For view v, both shift_rows[v, 0] and shift_rows[v, 1] equal -s_v floor((2 r - 4095) m_v / 4095) for row r, with a sign s_v of 1 or -1 and a whole magnitude m_v from 432 to 864; m_0 = 864. shift_columns[v, c] = s_v floor((2 c - 4095) 2 m_v / 4095) with the s_v and m_v of shift_rows.
All inputs are finite; a program needn't handle non-finite values.
Results may differ from a plain program's by a relative error of at most 0.018.
Values may be sent and summed in bfloat16 or wider, within the bound.
A program may use at most 64 MiB of HBM per device.

v0:
```python
import functools

import jax
import jax.numpy as jnp
import numpy as np
from jax import lax
from jax.experimental import pallas as pl
from jax.experimental.pallas import tpu as pltpu
from jax.sharding import PartitionSpec as P

BLOCK = 128
MARGIN = 32
WIN = BLOCK + 2 * MARGIN
HALF = WIN // 2
LINES = 16
ABSORB = 0.25
MESH = pl.DeviceIdType.MESH
BF = jnp.bfloat16
F32 = jnp.float32


def real_tables():
    q = np.arange(HALF + 1)
    p = np.arange(WIN)
    angle = (2.0 * np.pi * np.mod(p[:, None] * q[None, :], WIN).astype(np.float32) / WIN).astype(np.float32)
    forward = np.zeros((WIN, 256), np.float32)
    forward[:, : HALF + 1] = np.cos(angle)
    forward[:, 129 : 128 + HALF] = np.sin(angle)[:, 1:HALF]
    target = np.arange(BLOCK) + MARGIN
    angle = (2.0 * np.pi * np.mod(q[:, None] * target[None, :], WIN).astype(np.float32) / WIN).astype(np.float32)
    weight = np.where((q == 0) | (q == HALF), 1.0, 2.0)[:, None].astype(np.float32)
    inverse = np.zeros((256, BLOCK), np.float32)
    inverse[: HALF + 1] = weight * (np.cos(angle) / WIN)
    inverse[129 : 128 + HALF] = (2.0 * np.sin(angle) / WIN)[1:HALF]
    return forward, inverse


def iota(shape, dim):
    return lax.broadcasted_iota(jnp.int32, shape, dim)


def one_hot(mask):
    return jnp.where(mask, 1.0, 0.0).astype(BF)


def dot(a, b):
    return jnp.dot(a, b, preferred_element_type=F32)


def dot_nt(a, b):
    return lax.dot_general(a, b, (((1,), (1,)), ((), ())), preferred_element_type=F32)


def travel_phase(z, q):
    q = q.astype(F32)
    return (-2.0 * np.pi / (WIN * WIN)) * z * q * q


def kernel(
    nr, nc, vol, wa, wb, srs, scs, trav, sr, fr, sc, fc, fwd, inv, fwdt, invt,
    out_a, out_b,
    wbt, rows0, wrow_a, wrow_b, zone, o1, tile1, turn1, cols, o2, turn2, tile2, rows2, rot, ub, half, ext, extt,
    ramps, tabs, send, recv,
):
    r = lax.axis_index("row")
    c = lax.axis_index("col")
    tile_rows = nc * LINES
    quarters = tile_rows // BLOCK
    col_tiles = nc
    row_tiles = nr * quarters

    barrier = pltpu.get_barrier_semaphore()

    def greet_col(i, _):
        pl.semaphore_signal(barrier, inc=1, device_id={"col": lax.rem(c + i, nc)}, device_id_type=MESH)
        return 0

    def greet_row(i, _):
        pl.semaphore_signal(barrier, inc=1, device_id={"row": lax.rem(r + i, nr)}, device_id_type=MESH)
        return 0

    lax.fori_loop(1, nc, greet_col, 0)
    lax.fori_loop(1, nr, greet_row, 0)
    pl.semaphore_wait(barrier, nc + nr - 2)

    def sixteen(i):
        return pl.ds(pl.multiple_of(i * LINES, LINES), LINES)

    def to_col(phase, src, dst):
        def body(i, _):
            peer = lax.rem(c + i, nc)
            pltpu.make_async_remote_copy(
                src_ref=src(peer), dst_ref=dst, send_sem=send.at[phase], recv_sem=recv.at[phase],
                device_id={"col": peer}, device_id_type=MESH,
            ).start()
            return 0

        lax.fori_loop(1, nc, body, 0)

    def to_row(phase, src, dst):
        def body(i, _):
            peer = lax.rem(r + i, nr)
            pltpu.make_async_remote_copy(
                src_ref=src(peer), dst_ref=dst, send_sem=send.at[phase], recv_sem=recv.at[phase],
                device_id={"row": peer}, device_id_type=MESH,
            ).start()
            return 0

        lax.fori_loop(1, nr, body, 0)

    def arrived(phase, part):
        pltpu.make_async_copy(part, part, recv.at[phase]).wait()

    def left(phase, part):
        pltpu.make_async_copy(part, part, send.at[phase]).wait()

    to_col(0, lambda peer: vol.at[:, sixteen(peer), :], rows0.at[c])
    rows0[c] = vol[:, sixteen(c), :]

    eye = one_hot(iota((BLOCK, BLOCK), 0) == iota((BLOCK, BLOCK), 1))
    anti = one_hot(iota((BLOCK, BLOCK), 0) == BLOCK - 1 - iota((BLOCK, BLOCK), 1))

    lane = iota((LINES, 128), 1)

    def prepare(index, shifts, fractions, start, base, width):
        mine = iota((LINES, width), 1) == start + iota((LINES, width), 0)
        f = jnp.sum(jnp.where(mine, fractions, 0.0), axis=1, keepdims=True)
        k = jnp.sum(jnp.where(mine, shifts.astype(F32), 0.0), axis=1, keepdims=True)
        phase = (2.0 * np.pi / WIN) * f * lane.astype(F32)
        ramps[index, 0] = jnp.cos(phase)
        ramps[index, 1] = jnp.sin(phase)
        ramps[index, 2] = jnp.broadcast_to(k - base.astype(F32), (LINES, 128))
        offset = (-MARGIN - base) & 127
        pick = one_hot(iota((384, WIN), 0) - offset == iota((384, WIN), 1))
        tabs[index] = dot(pick, fwd[...]).astype(BF)

    def row_base(v, p):
        return jnp.minimum(srs[v, p, c * LINES], srs[v, p, c * LINES + LINES - 1])

    def col_base(v):
        return jnp.minimum(scs[v, r * LINES], scs[v, r * LINES + LINES - 1])

    for v in range(2):
        for p in range(2):
            prepare(3 * v + 2 * p, sr[v, pl.ds(p, 1), :], fr[v, pl.ds(p, 1), :], c * LINES, row_base(v, p), tile_rows)
        prepare(3 * v + 1, sc[pl.ds(v, 1), :], fc[pl.ds(v, 1), :], r * LINES, col_base(v), BLOCK)
    tabs[6] = dot(one_hot(iota((384, WIN), 0) - 96 == iota((384, WIN), 1)), fwd[...]).astype(BF)

    for part in range(2):
        flipped = dot(anti, wb[part]).astype(BF)
        for n in range(quarters):
            wbt[part, n * BLOCK : (n + 1) * BLOCK, :] = dot_nt(eye, flipped[:, n * BLOCK : (n + 1) * BLOCK]).astype(BF)

    zone[...] = jnp.zeros(zone.shape, BF)
    for v in range(2):
        ub[v, 0] = jnp.zeros((2, LINES, 128), BF)
        ub[v, col_tiles + 1] = jnp.zeros((2, LINES, 128), BF)

    pad = 14

    def shear(index, base, bits, src, count, dst):
        shift = ramps[index, 2].astype(jnp.int32)
        a = src[...].astype(F32)
        zero = jnp.zeros((1, 2, LINES, 128), F32)
        a = jnp.concatenate([a, zero], 0)
        for bit in range(bits):
            step = 2**bit
            turned = pltpu.roll(a, step, 3)
            before = jnp.concatenate([zero, turned[:-1]], 0)
            moved = jnp.where(lane >= step, turned, before)
            a = jnp.where((shift & step) != 0, moved, a)
        zone[pad : pad + count + 1] = a.astype(BF)
        first = lax.shift_right_arithmetic(-MARGIN - base, 7) + pad
        group = min(16, count)
        cosine = ramps[index, 0]
        sine = ramps[index, 1]

        def chunk(g, _):
            m = g * group
            pieces = [zone[pl.ds(first + m + i, group)].reshape(group * 2 * LINES, 128) for i in range(3)]
            spectrum = dot(jnp.concatenate(pieces, 1), tabs[index])
            even = spectrum[:, :128].reshape(group * 2, LINES, 128)
            odd = spectrum[:, 128:].reshape(group * 2, LINES, 128)
            y = jnp.concatenate([even * cosine - odd * sine, odd * cosine + even * sine], 2)
            line = dot(y.reshape(group * 2 * LINES, 256).astype(BF), inv[...])
            dst[pl.ds(m, group)] = line.reshape(group, 2, LINES, 128).astype(BF)
            return 0

        lax.fori_loop(0, count // group, chunk, 0)

    for v in range(2):
        if v == 0:
            arrived(0, rows0.at[pl.ds(0, nc - 1)])
        shear(3 * v, row_base(v, 0), 3, rows0, col_tiles, o1.at[v])
        to_col(3 + v, lambda peer, v=v: o1.at[v, peer], tile1.at[v, :, sixteen(c), :])
        tile1[v, :, sixteen(c), :] = o1[v, c]

    to_col(1, lambda peer: wa.at[:, sixteen(peer), :], wrow_a.at[c])
    wrow_a[c] = wa[:, sixteen(c), :]
    to_col(2, lambda peer: wbt.at[:, sixteen(peer), :], wrow_b.at[nc - 1 - c])
    wrow_b[nc - 1 - c] = wbt[:, sixteen(c), :]

    for v in range(2):
        arrived(3 + v, tile1.at[v, :, pl.ds(0, tile_rows - LINES), :])
        for part in range(2):
            t = dot_nt(eye, tile1[v, part]).astype(BF)
            for n in range(quarters):
                turn1[v, n, part] = t[:, n * BLOCK : (n + 1) * BLOCK]
        to_row(
            5 + v,
            lambda peer, v=v: turn1.at[v, :, :, sixteen(peer), :],
            cols.at[v, pl.ds(r * quarters, quarters)],
        )
        cols[v, pl.ds(r * quarters, quarters)] = turn1[v, :, :, sixteen(r), :]

    for v in range(2):
        arrived(5 + v, cols.at[v, pl.ds(0, row_tiles - quarters)])
        shear(3 * v + 1, col_base(v), 4, cols.at[v], row_tiles, o2.at[v])
        to_row(
            7 + v,
            lambda peer, v=v: o2.at[v, pl.ds(peer * quarters, quarters)],
            turn2.at[v, :, :, sixteen(r), :],
        )
        turn2[v, :, :, sixteen(r), :] = o2[v, pl.ds(r * quarters, quarters)]

    for v in range(2):
        arrived(7 + v, turn2.at[v, :, :, pl.ds(0, BLOCK - LINES), :])
        for part in range(2):
            for n in range(quarters):
                tile2[v, part, n * BLOCK : (n + 1) * BLOCK, :] = dot_nt(eye, turn2[v, n, part]).astype(BF)
        to_col(9 + v, lambda peer, v=v: tile2.at[v, :, sixteen(peer), :], rows2.at[v, c])
        rows2[v, c] = tile2[v, :, sixteen(c), :]

    for v in range(2):
        wave = (wrow_a, wrow_b)[v]
        arrived(9 + v, rows2.at[v, pl.ds(0, nc - 1)])
        shear(3 * v + 2, row_base(v, 1), 3, rows2.at[v], col_tiles, rot)
        arrived(1 + v, wave.at[pl.ds(0, nc - 1)])
        group = 4

        def through(g, _, v=v, wave=wave):
            m = g * group
            block = rot[pl.ds(m, group)].astype(F32)
            w = wave[pl.ds(m, group)].astype(F32)
            amplitude = jnp.exp(-ABSORB * block[:, 1])
            real = amplitude * jnp.cos(block[:, 0])
            imaginary = amplitude * jnp.sin(block[:, 0])
            ub[v, pl.ds(1 + m, group), 0] = (w[:, 0] * real - w[:, 1] * imaginary).astype(BF)
            ub[v, pl.ds(1 + m, group), 1] = (w[:, 0] * imaginary + w[:, 1] * real).astype(BF)
            return 0

        lax.fori_loop(0, col_tiles // group, through, 0)
        phase = travel_phase(trav[v], iota((1, 256), 1) & 127)
        factor_real = jnp.cos(phase)
        factor_imaginary = jnp.sin(phase)
        span = min(16, col_tiles)

        def travel(g, _, v=v, factor_real=factor_real, factor_imaginary=factor_imaginary):
            m = g * span
            pieces = [ub[v, pl.ds(m + i, span)].reshape(span * 2 * LINES, 128) for i in range(3)]
            spectrum = dot(jnp.concatenate(pieces, 1), tabs[6]).reshape(span, 2, LINES, 256)
            a, b = spectrum[:, 0], spectrum[:, 1]
            y = jnp.stack([factor_real * a - factor_imaginary * b, factor_real * b + factor_imaginary * a], 1)
            line = dot(y.reshape(span * 2 * LINES, 256).astype(BF), inv[...])
            half[v, pl.ds(m, span)] = line.reshape(span, 2, LINES, 128).astype(BF)
            return 0

        lax.fori_loop(0, col_tiles // span, travel, 0)
        spot = pl.ds(pl.multiple_of(MARGIN + c * LINES, LINES), LINES)
        if v == 0:
            to_col(11, lambda peer: half.at[0, peer], ext.at[0, :, spot, :])
            ext[0, :, spot, :] = half[0, c]
        else:
            to_col(12, lambda peer: half.at[1, nc - 1 - peer], ext.at[1, :, spot, :])
            ext[1, :, spot, :] = half[1, nc - 1 - c]

    top = pl.ds(0, MARGIN)
    bottom = pl.ds(MARGIN + tile_rows, MARGIN)
    head = pl.ds(MARGIN, MARGIN)
    tail = pl.ds(tile_rows, MARGIN)

    def down(v):
        return pltpu.make_async_remote_copy(
            src_ref=ext.at[v, :, tail, :], dst_ref=ext.at[v, :, top, :], send_sem=send.at[13 + v],
            recv_sem=recv.at[13 + v], device_id={"row": lax.rem(r + 1, nr)}, device_id_type=MESH,
        )

    def up(v):
        return pltpu.make_async_remote_copy(
            src_ref=ext.at[v, :, head, :], dst_ref=ext.at[v, :, bottom, :], send_sem=send.at[15 + v],
            recv_sem=recv.at[15 + v], device_id={"row": lax.rem(r + nr - 1, nr)}, device_id_type=MESH,
        )

    for v in range(2):
        arrived(11 + v, ext.at[v, :, pl.ds(0, tile_rows - LINES), :])

        @pl.when(r < nr - 1)
        def _(v=v):
            down(v).start()

        @pl.when(r > 0)
        def _(v=v):
            up(v).start()

        @pl.when(r == 0)
        def _(v=v):
            ext[v, :, top, :] = jnp.zeros((2, MARGIN, 128), BF)

        @pl.when(r == nr - 1)
        def _(v=v):
            ext[v, :, bottom, :] = jnp.zeros((2, MARGIN, 128), BF)

    for v in range(2):

        @pl.when(r > 0)
        def _(v=v):
            down(v).wait_recv()

        @pl.when(r < nr - 1)
        def _(v=v):
            up(v).wait_recv()

        if v == 0:
            phase = travel_phase(trav[0], iota((256, 128), 0) & 127)
            factor_real = jnp.cos(phase)
            factor_imaginary = jnp.sin(phase)
            for n in range(quarters):
                window = jnp.concatenate([ext[0, part, n * BLOCK : n * BLOCK + WIN, :] for part in range(2)], 1)
                spectrum = dot(fwdt[...], window)
                a, b = spectrum[:, :128], spectrum[:, 128:]
                y = jnp.concatenate(
                    [factor_real * a - factor_imaginary * b, factor_real * b + factor_imaginary * a], 1
                ).astype(BF)
                line = dot(invt[...], y).astype(BF)
                out_a[0, n * BLOCK : (n + 1) * BLOCK, :] = line[:, :128]
                out_a[1, n * BLOCK : (n + 1) * BLOCK, :] = line[:, 128:]
        else:
            phase = travel_phase(trav[1], iota((1, 256), 1) & 127)
            factor_real = jnp.cos(phase)
            factor_imaginary = jnp.sin(phase)
            for part in range(2):
                extt[part, :, 0 : tile_rows + 2 * MARGIN] = dot_nt(anti, ext[1, part]).astype(BF)
                extt[part, :, tile_rows + 2 * MARGIN :] = jnp.zeros((BLOCK, MARGIN * 2), BF)
            for n in range(quarters):
                window = extt[:, :, n * BLOCK : (n + 2) * BLOCK].reshape(2 * BLOCK, 2 * BLOCK)
                spectrum = dot(window[:, :WIN], fwd[...])
                a, b = spectrum[:BLOCK], spectrum[BLOCK:]
                y = jnp.concatenate(
                    [factor_real * a - factor_imaginary * b, factor_real * b + factor_imaginary * a], 0
                ).astype(BF)
                line = dot(y, inv[...]).astype(BF)
                out_b[0, :, n * BLOCK : (n + 1) * BLOCK] = line[:BLOCK]
                out_b[1, :, n * BLOCK : (n + 1) * BLOCK] = line[BLOCK:]

    left(0, vol.at[:, pl.ds(0, tile_rows - LINES), :])
    left(1, wa.at[:, pl.ds(0, tile_rows - LINES), :])
    left(2, wbt.at[:, pl.ds(0, tile_rows - LINES), :])
    for v in range(2):
        left(3 + v, o1.at[v, pl.ds(0, nc - 1)])
        left(5 + v, turn1.at[v, :, :, pl.ds(0, BLOCK - LINES), :])
        left(7 + v, o2.at[v, pl.ds(0, row_tiles - quarters)])
        left(9 + v, tile2.at[v, :, pl.ds(0, tile_rows - LINES), :])
        left(11 + v, half.at[v, pl.ds(0, nc - 1)])

        @pl.when(r < nr - 1)
        def _(v=v):
            down(v).wait_send()

        @pl.when(r > 0)
        def _(v=v):
            up(v).wait_send()


def on_device(nr, nc, vol, wa, wb, sr, fr, sc, fc, trav):
    forward, inverse = real_tables()
    tile_rows = nc * LINES
    quarters = tile_rows // BLOCK
    col_tiles, row_tiles = nc, nr * quarters
    vmem = pl.BlockSpec(memory_space=pltpu.VMEM)
    smem = pl.BlockSpec(memory_space=pltpu.SMEM)
    lines = (2, LINES, 128)
    scratch = [
        pltpu.VMEM((2, tile_rows, 128), BF),
        pltpu.VMEM((col_tiles, *lines), BF),
        pltpu.VMEM((col_tiles, *lines), BF),
        pltpu.VMEM((col_tiles, *lines), BF),
        pltpu.VMEM((64, *lines), BF),
        pltpu.VMEM((2, col_tiles, *lines), BF),
        pltpu.VMEM((2, 2, tile_rows, 128), BF),
        pltpu.VMEM((2, quarters, 2, BLOCK, 128), BF),
        pltpu.VMEM((2, row_tiles, *lines), BF),
        pltpu.VMEM((2, row_tiles, *lines), BF),
        pltpu.VMEM((2, quarters, 2, BLOCK, 128), BF),
        pltpu.VMEM((2, 2, tile_rows, 128), BF),
        pltpu.VMEM((2, col_tiles, *lines), BF),
        pltpu.VMEM((col_tiles, *lines), BF),
        pltpu.VMEM((2, col_tiles + 2, *lines), BF),
        pltpu.VMEM((2, col_tiles, *lines), BF),
        pltpu.VMEM((2, 2, tile_rows + 2 * MARGIN, 128), BF),
        pltpu.VMEM((2, BLOCK, tile_rows + BLOCK), BF),
        pltpu.VMEM((6, 3, LINES, 128), F32),
        pltpu.VMEM((7, 384, 256), BF),
        pltpu.SemaphoreType.DMA((17,)),
        pltpu.SemaphoreType.DMA((17,)),
    ]
    return pl.pallas_call(
        functools.partial(kernel, nr, nc),
        out_shape=(
            jax.ShapeDtypeStruct((2, tile_rows, 128), BF),
            jax.ShapeDtypeStruct((2, 128, tile_rows), BF),
        ),
        in_specs=[vmem] * 3 + [smem] * 3 + [vmem] * 8,
        out_specs=(vmem, vmem),
        scratch_shapes=scratch,
        compiler_params=pltpu.CompilerParams(
            collective_id=0, has_side_effects=True, vmem_limit_bytes=56 * 2**20
        ),
        name="rotate_travel",
    )(
        vol, wa, wb, sr, sc, trav, sr, fr, sc, fc,
        jnp.asarray(forward, BF), jnp.asarray(inverse, BF),
        jnp.asarray(forward.T, BF), jnp.asarray(inverse.T, BF),
    )


def solution(mesh):
    nr, nc = mesh.shape["row"], mesh.shape["col"]
    return jax.shard_map(
        functools.partial(on_device, nr, nc),
        mesh=mesh,
        in_specs=(
            P(None, "row", "col"),
            P(None, "row", "col"),
            P(None, "col", "row"),
            P(None, None, "row"),
            P(None, None, "row"),
            P(None, "col"),
            P(None, "col"),
            P(),
        ),
        out_specs=(P(None, "row", "col"), P(None, "col", "row")),
        check_vma=False,
    )
```

profile of v0, /device:TPU:8, one launch (start us, length us, event | category | flops | bytes accessed | tf_op | source)
XLA Modules:
  0.0 87.0 jit_solution(16306957227472326851)
XLA Ops:
  0.6 84.0 %rotate_travel.1 = (bf16[2,512,128]{2,1,0:T(8,128)(2,1)}, bf16[2,128,512]{2,1,0:T(8,128)(2,1)}) custom-call(bf16[2,512,128]{2,1,0:T(8,128)(2,1)} %vol.1, bf16[2,512,128]{2,1,0:T(8,128)(2,1)} %wa.1, bf16[2,128,512]{2,1,0:T(8,128)(2,1)} %wb.1, s32[2,2,512]{2,1,0:T(2,128)} %sr.1, s32[2,128]{1,0:T(2,128)} %sc.1, f32[2]{0:T(128)} %trav.1, s32[2,2,512]{2,1,0:T(2,128)} %sr.1, ...), custom_call_target="tpu_custom_call" | custom-call | tf_op jit(solution)/shard_map/rotate_travel/pallas_call | solution.py:406
  84.6 0.0 copy-start
  84.6 1.7 %copy.16 = bf16[2,512,128]{2,1,0:T(8,128)(2,1)} copy(bf16[2,512,128]{2,1,0:T(8,128)(2,1)} %get-tuple-element.4) | data formatting | bytes 524288
  86.3 0.0 copy-done
  86.3 0.7 copy.17
Async XLA Ops:
  84.6 1.7 %copy-start = (bf16[2,128,512]{2,1,0:T(8,128)(2,1)S(1)}, bf16[2,128,512]{2,1,0:T(8,128)(2,1)}, u32[]{:S(2)}) copy-start(bf16[2,128,512]{2,1,0:T(8,128)(2,1)} %get-tuple-element.5) | copy-start | bytes 786436
where the time goes:
time: 88.1 us; the launch traced here: 87 us
  Pallas kernels  84 us (95%)
  local copies, waits for them, and re-layouts  2.42 us (3%)
    pallas_call x1, Pallas kernels, on_device(): pl.pallas_call(functools.partial(kernel, nr, nc), out_shape=(jax.ShapeDty...  84 us
    unnamed x4, local copies, waits for them, and re-layouts  2.42 us

commit v1 on v0

--- a/solution.py
+++ b/solution.py
@@ -86,27 +86,54 @@
     def sixteen(i):
         return pl.ds(pl.multiple_of(i * LINES, LINES), LINES)
 
-    def to_col(phase, src, dst):
+    depth = nc // 4
+    width = nr // 2
+    zone_z, core = lax.rem(lax.div(c, 2), depth), lax.rem(c, 2)
+    side_c, side_r = lax.div(c, 2 * depth), lax.div(r, width)
+    place = lax.rem(r, width)
+
+    def hop(position, ring):
+        step = lax.div(position + 1, 2)
+        return jnp.where(lax.rem(position, 2) == 1, ring // 2 - step, ring // 2 + step)
+
+    def ship(src, dst, phase, landing, axis, peer):
+        pltpu.make_async_remote_copy(
+            src_ref=src(peer), dst_ref=dst, send_sem=send.at[phase], recv_sem=recv.at[landing],
+            device_id={axis: peer}, device_id_type=MESH,
+        ).start()
+
+    def to_col(phase, landing, src, dst, far):
+        base = (1 - side_c if far else side_c) * (2 * depth)
+
         def body(i, _):
-            peer = lax.rem(c + i, nc)
-            pltpu.make_async_remote_copy(
-                src_ref=src(peer), dst_ref=dst, send_sem=send.at[phase], recv_sem=recv.at[phase],
-                device_id={"col": peer}, device_id_type=MESH,
-            ).start()
+            stem = base + 2 * lax.rem(zone_z + hop(i, depth), depth)
+            ship(src, dst, phase, landing, "col", stem + 1 - core)
+            ship(src, dst, phase, landing, "col", stem + core)
             return 0
 
-        lax.fori_loop(1, nc, body, 0)
-
-    def to_row(phase, src, dst):
+        lax.fori_loop(0, depth if far else depth - 1, body, 0)
+        if not far:
+            ship(src, dst, phase, landing, "col", base + 2 * zone_z + 1 - core)
+
+    def to_row(phase, landing, src, dst, far):
+        base = (1 - side_r if far else side_r) * width
+
         def body(i, _):
-            peer = lax.rem(r + i, nr)
-            pltpu.make_async_remote_copy(
-                src_ref=src(peer), dst_ref=dst, send_sem=send.at[phase], recv_sem=recv.at[phase],
-                device_id={"row": peer}, device_id_type=MESH,
-            ).start()
+            ship(src, dst, phase, landing, "row", base + lax.rem(place + hop(i, width), width))
             return 0
 
-        lax.fori_loop(1, nr, body, 0)
+        lax.fori_loop(0, width if far else width - 1, body, 0)
+
+    def to_quarter(phase, landing, src, dst, quarter, own):
+        def body(i, _):
+            ship(src, dst, phase, landing, "col", quarter * depth + lax.rem(lax.rem(c, depth) + depth - i, depth))
+            return 0
+
+        lax.fori_loop(1 if own else 0, depth, body, 0)
+
+    near = lax.div(c, depth)
+    order = [(1 - lax.div(near, 2)) * 2 + (1 - lax.rem(near, 2)), (1 - lax.div(near, 2)) * 2 + lax.rem(near, 2),
+             lax.div(near, 2) * 2 + (1 - lax.rem(near, 2)), near]
 
     def arrived(phase, part):
         pltpu.make_async_copy(part, part, recv.at[phase]).wait()
@@ -114,13 +141,26 @@
     def left(phase, part):
         pltpu.make_async_copy(part, part, send.at[phase]).wait()
 
-    to_col(0, lambda peer: vol.at[:, sixteen(peer), :], rows0.at[c])
+    for far in (True, False):
+        to_col(0, 0, lambda peer: vol.at[:, sixteen(peer), :], rows0.at[c], far)
     rows0[c] = vol[:, sixteen(c), :]
 
     eye = one_hot(iota((BLOCK, BLOCK), 0) == iota((BLOCK, BLOCK), 1))
     anti = one_hot(iota((BLOCK, BLOCK), 0) == BLOCK - 1 - iota((BLOCK, BLOCK), 1))
 
     lane = iota((LINES, 128), 1)
+
+    def table(offset):
+        row = iota((256, WIN), 0) - offset
+        row = jnp.where(iota((256, WIN), 0) < offset - 64, row + 256, row)
+        return dot(one_hot(row == iota((256, WIN), 1)), fwd[...]).astype(BF)
+
+    def merged(ref, start, count, offset):
+        outer = jnp.where(
+            iota((1, 1, LINES, 128), 3) < offset - 64, ref[pl.ds(start + 2, count)], ref[pl.ds(start, count)]
+        )
+        middle = ref[pl.ds(start + 1, count)]
+        return jnp.concatenate([t.reshape(count * 2 * LINES, 128) for t in (outer, middle)], 1)
 
     def prepare(index, shifts, fractions, start, base, width):
         mine = iota((LINES, width), 1) == start + iota((LINES, width), 0)
@@ -131,8 +171,7 @@
         ramps[index, 1] = jnp.sin(phase)
         ramps[index, 2] = jnp.broadcast_to(k - base.astype(F32), (LINES, 128))
         offset = (-MARGIN - base) & 127
-        pick = one_hot(iota((384, WIN), 0) - offset == iota((384, WIN), 1))
-        tabs[index] = dot(pick, fwd[...]).astype(BF)
+        tabs[index] = table(offset)
 
     def row_base(v, p):
         return jnp.minimum(srs[v, p, c * LINES], srs[v, p, c * LINES + LINES - 1])
@@ -144,7 +183,7 @@
         for p in range(2):
             prepare(3 * v + 2 * p, sr[v, pl.ds(p, 1), :], fr[v, pl.ds(p, 1), :], c * LINES, row_base(v, p), tile_rows)
         prepare(3 * v + 1, sc[pl.ds(v, 1), :], fc[pl.ds(v, 1), :], r * LINES, col_base(v), BLOCK)
-    tabs[6] = dot(one_hot(iota((384, WIN), 0) - 96 == iota((384, WIN), 1)), fwd[...]).astype(BF)
+    tabs[6] = table(jnp.int32(96))
 
     for part in range(2):
         flipped = dot(anti, wb[part]).astype(BF)
@@ -158,7 +197,7 @@
 
     pad = 14
 
-    def shear(index, base, bits, src, count, dst):
+    def shear(index, base, bits, src, count, dst, side, after):
         shift = ramps[index, 2].astype(jnp.int32)
         a = src[...].astype(F32)
         zero = jnp.zeros((1, 2, LINES, 128), F32)
@@ -171,70 +210,83 @@
             a = jnp.where((shift & step) != 0, moved, a)
         zone[pad : pad + count + 1] = a.astype(BF)
         first = lax.shift_right_arithmetic(-MARGIN - base, 7) + pad
-        group = min(16, count)
+        offset = (-MARGIN - base) & 127
         cosine = ramps[index, 0]
         sine = ramps[index, 1]
-
-        def chunk(g, _):
-            m = g * group
-            pieces = [zone[pl.ds(first + m + i, group)].reshape(group * 2 * LINES, 128) for i in range(3)]
-            spectrum = dot(jnp.concatenate(pieces, 1), tabs[index])
+        group = count // 2
+        for far in (True, False):
+            m = (1 - side if far else side) * group
+            spectrum = dot(merged(zone, first + m, group, offset), tabs[index])
             even = spectrum[:, :128].reshape(group * 2, LINES, 128)
             odd = spectrum[:, 128:].reshape(group * 2, LINES, 128)
             y = jnp.concatenate([even * cosine - odd * sine, odd * cosine + even * sine], 2)
             line = dot(y.reshape(group * 2 * LINES, 256).astype(BF), inv[...])
             dst[pl.ds(m, group)] = line.reshape(group, 2, LINES, 128).astype(BF)
-            return 0
-
-        lax.fori_loop(0, count // group, chunk, 0)
+            after(far)
 
     for v in range(2):
         if v == 0:
             arrived(0, rows0.at[pl.ds(0, nc - 1)])
-        shear(3 * v, row_base(v, 0), 3, rows0, col_tiles, o1.at[v])
-        to_col(3 + v, lambda peer, v=v: o1.at[v, peer], tile1.at[v, :, sixteen(c), :])
+
+        def after(far, v=v):
+            to_col(3 + v, 17 + 4 * v + near, lambda peer: o1.at[v, peer], tile1.at[v, :, sixteen(c), :], far)
+
+        shear(3 * v, row_base(v, 0), 3, rows0, col_tiles, o1.at[v], side_c, after)
         tile1[v, :, sixteen(c), :] = o1[v, c]
 
-    to_col(1, lambda peer: wa.at[:, sixteen(peer), :], wrow_a.at[c])
+    def landed(landing, part, own):
+        def wait(number):
+            whole = part.at[:, pl.ds(0, number * LINES), :]
+            pltpu.make_async_copy(whole, whole, recv.at[landing]).wait()
+
+        wait(depth - 1 if own else depth)
+
+    for v in range(2):
+        for i, k in enumerate(order):
+            spot = pl.ds(pl.multiple_of(k * BLOCK, BLOCK), BLOCK)
+            landed(17 + 4 * v + k, tile1.at[v], i == 3)
+            for part in range(2):
+                turn1[v, k, part] = dot_nt(eye, tile1[v, part, spot, :]).astype(BF)
+            for far in (True, False):
+                to_row(
+                    5 + v, 5 + v, lambda peer, v=v, k=k: turn1.at[v, k, :, sixteen(peer), :],
+                    cols.at[v, r * quarters + k], far,
+                )
+            cols[v, r * quarters + k] = turn1[v, k, :, sixteen(r), :]
+        for far in (True, False):
+            if v == 0:
+                to_col(1, 1, lambda peer: wa.at[:, sixteen(peer), :], wrow_a.at[c], far)
+            else:
+                to_col(2, 2, lambda peer: wbt.at[:, sixteen(peer), :], wrow_b.at[nc - 1 - c], far)
     wrow_a[c] = wa[:, sixteen(c), :]
-    to_col(2, lambda peer: wbt.at[:, sixteen(peer), :], wrow_b.at[nc - 1 - c])
     wrow_b[nc - 1 - c] = wbt[:, sixteen(c), :]
 
     for v in range(2):
-        arrived(3 + v, tile1.at[v, :, pl.ds(0, tile_rows - LINES), :])
-        for part in range(2):
-            t = dot_nt(eye, tile1[v, part]).astype(BF)
-            for n in range(quarters):
-                turn1[v, n, part] = t[:, n * BLOCK : (n + 1) * BLOCK]
-        to_row(
-            5 + v,
-            lambda peer, v=v: turn1.at[v, :, :, sixteen(peer), :],
-            cols.at[v, pl.ds(r * quarters, quarters)],
-        )
-        cols[v, pl.ds(r * quarters, quarters)] = turn1[v, :, :, sixteen(r), :]
-
-    for v in range(2):
         arrived(5 + v, cols.at[v, pl.ds(0, row_tiles - quarters)])
-        shear(3 * v + 1, col_base(v), 4, cols.at[v], row_tiles, o2.at[v])
-        to_row(
-            7 + v,
-            lambda peer, v=v: o2.at[v, pl.ds(peer * quarters, quarters)],
-            turn2.at[v, :, :, sixteen(r), :],
-        )
+
+        def after(far, v=v):
+            for k in order:
+                to_row(
+                    7 + v, 25 + 4 * v + k, lambda peer, k=k: o2.at[v, peer * quarters + k],
+                    turn2.at[v, k, :, sixteen(r), :], far,
+                )
+
+        shear(3 * v + 1, col_base(v), 4, cols.at[v], row_tiles, o2.at[v], side_r, after)
         turn2[v, :, :, sixteen(r), :] = o2[v, pl.ds(r * quarters, quarters)]
 
     for v in range(2):
-        arrived(7 + v, turn2.at[v, :, :, pl.ds(0, BLOCK - LINES), :])
-        for part in range(2):
-            for n in range(quarters):
-                tile2[v, part, n * BLOCK : (n + 1) * BLOCK, :] = dot_nt(eye, turn2[v, n, part]).astype(BF)
-        to_col(9 + v, lambda peer, v=v: tile2.at[v, :, sixteen(peer), :], rows2.at[v, c])
+        for i, k in enumerate(order):
+            spot = pl.ds(pl.multiple_of(k * BLOCK, BLOCK), BLOCK)
+            arrived(25 + 4 * v + k, turn2.at[v, 0, :, pl.ds(0, BLOCK - LINES), :])
+            for part in range(2):
+                tile2[v, part, spot, :] = dot_nt(eye, turn2[v, k, part]).astype(BF)
+            to_quarter(9 + v, 9 + v, lambda peer, v=v: tile2.at[v, :, sixteen(peer), :], rows2.at[v, c], k, i == 3)
         rows2[v, c] = tile2[v, :, sixteen(c), :]
 
     for v in range(2):
         wave = (wrow_a, wrow_b)[v]
         arrived(9 + v, rows2.at[v, pl.ds(0, nc - 1)])
-        shear(3 * v + 2, row_base(v, 1), 3, rows2.at[v], col_tiles, rot)
+        shear(3 * v + 2, row_base(v, 1), 3, rows2.at[v], col_tiles, rot, side_c, lambda far: None)
         arrived(1 + v, wave.at[pl.ds(0, nc - 1)])
         group = 4
 
@@ -253,26 +305,20 @@
         phase = travel_phase(trav[v], iota((1, 256), 1) & 127)
         factor_real = jnp.cos(phase)
         factor_imaginary = jnp.sin(phase)
-        span = min(16, col_tiles)
-
-        def travel(g, _, v=v, factor_real=factor_real, factor_imaginary=factor_imaginary):
-            m = g * span
-            pieces = [ub[v, pl.ds(m + i, span)].reshape(span * 2 * LINES, 128) for i in range(3)]
-            spectrum = dot(jnp.concatenate(pieces, 1), tabs[6]).reshape(span, 2, LINES, 256)
+        span = col_tiles // 2
+        spot = pl.ds(pl.multiple_of(MARGIN + c * LINES, LINES), LINES)
+        for far in (True, False):
+            m = (side_c if far == (v == 1) else 1 - side_c) * span
+            spectrum = dot(merged(ub.at[v], m, span, 96), tabs[6]).reshape(span, 2, LINES, 256)
             a, b = spectrum[:, 0], spectrum[:, 1]
             y = jnp.stack([factor_real * a - factor_imaginary * b, factor_real * b + factor_imaginary * a], 1)
             line = dot(y.reshape(span * 2 * LINES, 256).astype(BF), inv[...])
             half[v, pl.ds(m, span)] = line.reshape(span, 2, LINES, 128).astype(BF)
-            return 0
-
-        lax.fori_loop(0, col_tiles // span, travel, 0)
-        spot = pl.ds(pl.multiple_of(MARGIN + c * LINES, LINES), LINES)
-        if v == 0:
-            to_col(11, lambda peer: half.at[0, peer], ext.at[0, :, spot, :])
-            ext[0, :, spot, :] = half[0, c]
-        else:
-            to_col(12, lambda peer: half.at[1, nc - 1 - peer], ext.at[1, :, spot, :])
-            ext[1, :, spot, :] = half[1, nc - 1 - c]
+            if v == 0:
+                to_col(11, 33 + near, lambda peer: half.at[0, peer], ext.at[0, :, spot, :], far)
+            else:
+                to_col(12, 37 + near, lambda peer: half.at[1, nc - 1 - peer], ext.at[1, :, spot, :], far)
+        ext[v, :, spot, :] = half[v, c if v == 0 else nc - 1 - c]
 
     top = pl.ds(0, MARGIN)
     bottom = pl.ds(MARGIN + tile_rows, MARGIN)
@@ -292,7 +338,15 @@
         )
 
     for v in range(2):
-        arrived(11 + v, ext.at[v, :, pl.ds(0, tile_rows - LINES), :])
+        for k in range(4):
+
+            @pl.when(near == k)
+            def _(v=v, k=k):
+                landed(33 + 4 * v + k, ext.at[v], True)
+
+            @pl.when(near != k)
+            def _(v=v, k=k):
+                landed(33 + 4 * v + k, ext.at[v], False)
 
         @pl.when(r < nr - 1)
         def _(v=v):
@@ -309,8 +363,6 @@
         @pl.when(r == nr - 1)
         def _(v=v):
             ext[v, :, bottom, :] = jnp.zeros((2, MARGIN, 128), BF)
-
-    for v in range(2):
 
         @pl.when(r > 0)
         def _(v=v):
@@ -399,9 +451,9 @@
         pltpu.VMEM((2, 2, tile_rows + 2 * MARGIN, 128), BF),
         pltpu.VMEM((2, BLOCK, tile_rows + BLOCK), BF),
         pltpu.VMEM((6, 3, LINES, 128), F32),
-        pltpu.VMEM((7, 384, 256), BF),
+        pltpu.VMEM((7, 256, 256), BF),
         pltpu.SemaphoreType.DMA((17,)),
-        pltpu.SemaphoreType.DMA((17,)),
+        pltpu.SemaphoreType.DMA((41,)),
     ]
     return pl.pallas_call(
         functools.partial(kernel, nr, nc),

time: 88.1 us -> 81.5 us (0.925); the launches traced: 87 us -> 81.4 us
  Pallas kernels: 84 us -> 78.3 us
    pallas_call x1, Pallas kernels: 84 us -> 78.3 us  [on_device(): pl.pallas_call(functools.partial(kernel, nr, nc), out_shape=(jax.ShapeDty...]
where the time goes in v1:
time: 81.5 us; the launch traced here: 81.4 us
  Pallas kernels  78.3 us (96%)
  local copies, waits for them, and re-layouts  2.42 us (3%)
    pallas_call x1, Pallas kernels, on_device(): pl.pallas_call(functools.partial(kernel, nr, nc), out_shape=(jax.ShapeDty...  78.3 us
    unnamed x4, local copies, waits for them, and re-layouts  2.42 us

profile of v1, /device:TPU:8, one launch (start us, length us, event | category | flops | bytes accessed | tf_op | source)
XLA Modules:
  0.0 81.4 jit_solution(5902446756118803212)
XLA Ops:
  0.6 78.3 %rotate_travel.1 = (bf16[2,512,128]{2,1,0:T(8,128)(2,1)}, bf16[2,128,512]{2,1,0:T(8,128)(2,1)}) custom-call(bf16[2,512,128]{2,1,0:T(8,128)(2,1)} %vol.1, bf16[2,512,128]{2,1,0:T(8,128)(2,1)} %wa.1, bf16[2,128,512]{2,1,0:T(8,128)(2,1)} %wb.1, s32[2,2,512]{2,1,0:T(2,128)} %sr.1, s32[2,128]{1,0:T(2,128)} %sc.1, f32[2]{0:T(128)} %trav.1, s32[2,2,512]{2,1,0:T(2,128)} %sr.1, ...), custom_call_target="tpu_custom_call" | custom-call | tf_op jit(solution)/shard_map/rotate_travel/pallas_call | solution.py:458
  79.0 0.0 copy-start
  79.0 1.7 %copy.16 = bf16[2,512,128]{2,1,0:T(8,128)(2,1)} copy(bf16[2,512,128]{2,1,0:T(8,128)(2,1)} %get-tuple-element.4) | data formatting | bytes 524288
  80.7 0.0 copy-done
  80.7 0.7 copy.17
Async XLA Ops:
  79.0 1.7 %copy-start = (bf16[2,128,512]{2,1,0:T(8,128)(2,1)S(1)}, bf16[2,128,512]{2,1,0:T(8,128)(2,1)}, u32[]{:S(2)}) copy-start(bf16[2,128,512]{2,1,0:T(8,128)(2,1)} %get-tuple-element.5) | copy-start | bytes 786436

commit v2 on v1

--- a/solution.py
+++ b/solution.py
@@ -51,15 +51,33 @@
     return lax.dot_general(a, b, (((1,), (1,)), ((), ())), preferred_element_type=F32)
 
 
+def cos_sin(x):
+    turns = jnp.floor(x * np.float32(2.0 / np.pi) + 0.5)
+    y = ((x - turns * np.float32(1.5703125)) - turns * np.float32(4.837512969970703125e-4)) - turns * np.float32(
+        7.54978995489188216e-8
+    )
+    z = y * y
+    sine = y + y * z * (np.float32(-1.6666654611e-1) + z * (np.float32(8.3321608736e-3) + z * np.float32(-1.9515295891e-4)))
+    cosine = 1.0 - 0.5 * z + z * z * (
+        np.float32(4.166664568298827e-2) + z * (np.float32(-1.388731625493765e-3) + z * np.float32(2.443315711809948e-5))
+    )
+    quarter = turns.astype(jnp.int32)
+    swap = (quarter & 1) == 1
+    real, imaginary = jnp.where(swap, sine, cosine), jnp.where(swap, cosine, sine)
+    real = jnp.where(((quarter + 1) & 2) == 2, -real, real)
+    return real, jnp.where((quarter & 2) == 2, -imaginary, imaginary)
+
+
 def travel_phase(z, q):
     q = q.astype(F32)
     return (-2.0 * np.pi / (WIN * WIN)) * z * q * q
 
 
 def kernel(
-    nr, nc, vol, wa, wb, srs, scs, trav, sr, fr, sc, fc, fwd, inv, fwdt, invt,
+    nr, nc, vol_in, wa_in, wb_in, sr_in, fr_in, sc_in, fc_in, trav_in, fwd_in, inv_in, fwdt_in, invt_in,
     out_a, out_b,
-    wbt, rows0, wrow_a, wrow_b, zone, o1, tile1, turn1, cols, o2, turn2, tile2, rows2, rot, ub, half, ext, extt,
+    vol, wa, wb, srs, scs, trav, sr, fr, sc, fc, fwd, inv, fwdt, invt, load,
+    wbt, rows0, wrow_a, wrow_b, zone, o1, tile1, turn1, cols, o2, turn2, tile2, rows2, rot, ub, half, ext,
     ramps, tabs, send, recv,
 ):
     r = lax.axis_index("row")
@@ -81,6 +99,16 @@
 
     lax.fori_loop(1, nc, greet_col, 0)
     lax.fori_loop(1, nr, greet_row, 0)
+    loads = [
+        pltpu.make_async_copy(src, dst, load.at[i])
+        for i, (src, dst) in enumerate([
+            (vol_in, vol), (wa_in, wa), (wb_in, wb), (sr_in, srs), (sc_in, scs), (trav_in, trav), (sr_in, sr), (fr_in, fr), (sc_in, sc),
+            (fc_in, fc), (fwd_in, fwd), (inv_in, inv), (fwdt_in, fwdt), (invt_in, invt),
+        ])
+    ]
+    for copy in loads:
+        copy.start()
+    loads[0].wait()
     pl.semaphore_wait(barrier, nc + nr - 2)
 
     def sixteen(i):
@@ -92,9 +120,9 @@
     side_c, side_r = lax.div(c, 2 * depth), lax.div(r, width)
     place = lax.rem(r, width)
 
-    def hop(position, ring):
-        step = lax.div(position + 1, 2)
-        return jnp.where(lax.rem(position, 2) == 1, ring // 2 - step, ring // 2 + step)
+    def hops(ring):
+        far = ring // 2
+        return [far - (i + 1) // 2 if i % 2 else far + i // 2 for i in range(ring)]
 
     def ship(src, dst, phase, landing, axis, peer):
         pltpu.make_async_remote_copy(
@@ -104,32 +132,22 @@
 
     def to_col(phase, landing, src, dst, far):
         base = (1 - side_c if far else side_c) * (2 * depth)
-
-        def body(i, _):
-            stem = base + 2 * lax.rem(zone_z + hop(i, depth), depth)
+        for step in hops(depth):
+            stem = base + 2 * lax.rem(zone_z + step, depth)
             ship(src, dst, phase, landing, "col", stem + 1 - core)
-            ship(src, dst, phase, landing, "col", stem + core)
-            return 0
-
-        lax.fori_loop(0, depth if far else depth - 1, body, 0)
-        if not far:
-            ship(src, dst, phase, landing, "col", base + 2 * zone_z + 1 - core)
+            if far or step:
+                ship(src, dst, phase, landing, "col", stem + core)
 
     def to_row(phase, landing, src, dst, far):
         base = (1 - side_r if far else side_r) * width
-
-        def body(i, _):
-            ship(src, dst, phase, landing, "row", base + lax.rem(place + hop(i, width), width))
-            return 0
-
-        lax.fori_loop(0, width if far else width - 1, body, 0)
+        for step in hops(width):
+            if far or step:
+                ship(src, dst, phase, landing, "row", base + lax.rem(place + step, width))
 
     def to_quarter(phase, landing, src, dst, quarter, own):
-        def body(i, _):
-            ship(src, dst, phase, landing, "col", quarter * depth + lax.rem(lax.rem(c, depth) + depth - i, depth))
-            return 0
-
-        lax.fori_loop(1 if own else 0, depth, body, 0)
+        for step in range(1 if own else 0, depth):
+            peer = quarter * depth + lax.rem(lax.rem(c, depth) + depth - step, depth)
+            ship(src, dst, phase, landing, "col", peer)
 
     near = lax.div(c, depth)
     order = [(1 - lax.div(near, 2)) * 2 + (1 - lax.rem(near, 2)), (1 - lax.div(near, 2)) * 2 + lax.rem(near, 2),
@@ -141,9 +159,18 @@
     def left(phase, part):
         pltpu.make_async_copy(part, part, send.at[phase]).wait()
 
+    def send_wave(v, far):
+        if v == 0:
+            to_col(1, 1, lambda peer: wa.at[:, sixteen(peer), :], wrow_a.at[c], far)
+        else:
+            to_col(2, 2, lambda peer: wbt.at[:, sixteen(peer), :], wrow_b.at[nc - 1 - c], far)
+
     for far in (True, False):
         to_col(0, 0, lambda peer: vol.at[:, sixteen(peer), :], rows0.at[c], far)
+    for copy in loads[1:]:
+        copy.wait()
     rows0[c] = vol[:, sixteen(c), :]
+    wrow_a[c] = wa[:, sixteen(c), :]
 
     eye = one_hot(iota((BLOCK, BLOCK), 0) == iota((BLOCK, BLOCK), 1))
     anti = one_hot(iota((BLOCK, BLOCK), 0) == BLOCK - 1 - iota((BLOCK, BLOCK), 1))
@@ -224,6 +251,7 @@
             dst[pl.ds(m, group)] = line.reshape(group, 2, LINES, 128).astype(BF)
             after(far)
 
+    send_wave(0, True)
     for v in range(2):
         if v == 0:
             arrived(0, rows0.at[pl.ds(0, nc - 1)])
@@ -241,7 +269,7 @@
 
         wait(depth - 1 if own else depth)
 
-    for v in range(2):
+    def rows_to_columns(v):
         for i, k in enumerate(order):
             spot = pl.ds(pl.multiple_of(k * BLOCK, BLOCK), BLOCK)
             landed(17 + 4 * v + k, tile1.at[v], i == 3)
@@ -249,39 +277,41 @@
                 turn1[v, k, part] = dot_nt(eye, tile1[v, part, spot, :]).astype(BF)
             for far in (True, False):
                 to_row(
-                    5 + v, 5 + v, lambda peer, v=v, k=k: turn1.at[v, k, :, sixteen(peer), :],
-                    cols.at[v, r * quarters + k], far,
+                    5 + v, 5 + v, lambda peer: turn1.at[v, k, :, sixteen(peer), :], cols.at[v, r * quarters + k], far
                 )
             cols[v, r * quarters + k] = turn1[v, k, :, sixteen(r), :]
-        for far in (True, False):
-            if v == 0:
-                to_col(1, 1, lambda peer: wa.at[:, sixteen(peer), :], wrow_a.at[c], far)
-            else:
-                to_col(2, 2, lambda peer: wbt.at[:, sixteen(peer), :], wrow_b.at[nc - 1 - c], far)
-    wrow_a[c] = wa[:, sixteen(c), :]
-    wrow_b[nc - 1 - c] = wbt[:, sixteen(c), :]
-
-    for v in range(2):
+
+    def shear_columns(v):
         arrived(5 + v, cols.at[v, pl.ds(0, row_tiles - quarters)])
 
-        def after(far, v=v):
-            for k in order:
+        shear(3 * v + 1, col_base(v), 4, cols.at[v], row_tiles, o2.at[v], side_r, lambda far: None)
+        for k in order:
+            for far in (True, False):
                 to_row(
-                    7 + v, 25 + 4 * v + k, lambda peer, k=k: o2.at[v, peer * quarters + k],
+                    7 + v, 25 + 4 * v + k, lambda peer: o2.at[v, peer * quarters + k],
                     turn2.at[v, k, :, sixteen(r), :], far,
                 )
-
-        shear(3 * v + 1, col_base(v), 4, cols.at[v], row_tiles, o2.at[v], side_r, after)
         turn2[v, :, :, sixteen(r), :] = o2[v, pl.ds(r * quarters, quarters)]
 
-    for v in range(2):
+    def columns_to_rows(v):
         for i, k in enumerate(order):
             spot = pl.ds(pl.multiple_of(k * BLOCK, BLOCK), BLOCK)
             arrived(25 + 4 * v + k, turn2.at[v, 0, :, pl.ds(0, BLOCK - LINES), :])
             for part in range(2):
                 tile2[v, part, spot, :] = dot_nt(eye, turn2[v, k, part]).astype(BF)
-            to_quarter(9 + v, 9 + v, lambda peer, v=v: tile2.at[v, :, sixteen(peer), :], rows2.at[v, c], k, i == 3)
+            to_quarter(9 + v, 9 + v, lambda peer: tile2.at[v, :, sixteen(peer), :], rows2.at[v, c], k, i == 3)
         rows2[v, c] = tile2[v, :, sixteen(c), :]
+
+    wrow_b[nc - 1 - c] = wbt[:, sixteen(c), :]
+    rows_to_columns(0)
+    send_wave(0, False)
+    send_wave(1, False)
+    rows_to_columns(1)
+    shear_columns(0)
+    columns_to_rows(0)
+    shear_columns(1)
+    send_wave(1, True)
+    columns_to_rows(1)
 
     for v in range(2):
         wave = (wrow_a, wrow_b)[v]
@@ -295,8 +325,9 @@
             block = rot[pl.ds(m, group)].astype(F32)
             w = wave[pl.ds(m, group)].astype(F32)
             amplitude = jnp.exp(-ABSORB * block[:, 1])
-            real = amplitude * jnp.cos(block[:, 0])
-            imaginary = amplitude * jnp.sin(block[:, 0])
+            cosine, sine = cos_sin(block[:, 0])
+            real = amplitude * cosine
+            imaginary = amplitude * sine
             ub[v, pl.ds(1 + m, group), 0] = (w[:, 0] * real - w[:, 1] * imaginary).astype(BF)
             ub[v, pl.ds(1 + m, group), 1] = (w[:, 0] * imaginary + w[:, 1] * real).astype(BF)
             return 0
@@ -337,8 +368,33 @@
             recv_sem=recv.at[15 + v], device_id={"row": lax.rem(r + nr - 1, nr)}, device_id_type=MESH,
         )
 
+    phase = travel_phase(trav[0], iota((256, 128), 0) & 127)
+    down_real, down_imaginary = jnp.cos(phase), jnp.sin(phase)
+    phase = travel_phase(trav[1], iota((1, 256), 1) & 127)
+    along_real, along_imaginary = jnp.cos(phase), jnp.sin(phase)
+
+    def finish(v, n):
+        rows = slice(n * BLOCK, n * BLOCK + WIN)
+        spot = slice(n * BLOCK, (n + 1) * BLOCK)
+        if v == 0:
+            window = jnp.concatenate([ext[0, part, rows, :] for part in range(2)], 1)
+            spectrum = dot(fwdt[...], window)
+            a, b = spectrum[:, :128], spectrum[:, 128:]
+            y = jnp.concatenate([down_real * a - down_imaginary * b, down_real * b + down_imaginary * a], 1)
+            line = dot(invt[...], y.astype(BF)).astype(BF)
+            out_a[0, spot, :] = line[:, :128]
+            out_a[1, spot, :] = line[:, 128:]
+        else:
+            window = jnp.concatenate([dot_nt(anti, ext[1, part, rows, :]).astype(BF) for part in range(2)], 0)
+            spectrum = dot(window, fwd[...])
+            a, b = spectrum[:BLOCK], spectrum[BLOCK:]
+            y = jnp.concatenate([along_real * a - along_imaginary * b, along_real * b + along_imaginary * a], 0)
+            line = dot(y.astype(BF), inv[...]).astype(BF)
+            out_b[0, :, spot] = line[:BLOCK]
+            out_b[1, :, spot] = line[BLOCK:]
+
     for v in range(2):
-        for k in range(4):
+        for k in (0, quarters - 1, *range(1, quarters - 1)):
 
             @pl.when(near == k)
             def _(v=v, k=k):
@@ -348,61 +404,40 @@
             def _(v=v, k=k):
                 landed(33 + 4 * v + k, ext.at[v], False)
 
-        @pl.when(r < nr - 1)
-        def _(v=v):
-            down(v).start()
-
-        @pl.when(r > 0)
-        def _(v=v):
-            up(v).start()
-
-        @pl.when(r == 0)
-        def _(v=v):
-            ext[v, :, top, :] = jnp.zeros((2, MARGIN, 128), BF)
-
-        @pl.when(r == nr - 1)
-        def _(v=v):
-            ext[v, :, bottom, :] = jnp.zeros((2, MARGIN, 128), BF)
+            if k == 0:
+
+                @pl.when(r > 0)
+                def _(v=v):
+                    up(v).start()
+
+                @pl.when(r == 0)
+                def _(v=v):
+                    ext[v, :, top, :] = jnp.zeros((2, MARGIN, 128), BF)
+
+            if k == quarters - 1:
+
+                @pl.when(r < nr - 1)
+                def _(v=v):
+                    down(v).start()
+
+                @pl.when(r == nr - 1)
+                def _(v=v):
+                    ext[v, :, bottom, :] = jnp.zeros((2, MARGIN, 128), BF)
+
+        for n in range(1, quarters - 1):
+            finish(v, n)
 
         @pl.when(r > 0)
         def _(v=v):
             down(v).wait_recv()
 
+        finish(v, 0)
+
         @pl.when(r < nr - 1)
         def _(v=v):
             up(v).wait_recv()
 
-        if v == 0:
-            phase = travel_phase(trav[0], iota((256, 128), 0) & 127)
-            factor_real = jnp.cos(phase)
-            factor_imaginary = jnp.sin(phase)
-            for n in range(quarters):
-                window = jnp.concatenate([ext[0, part, n * BLOCK : n * BLOCK + WIN, :] for part in range(2)], 1)
-                spectrum = dot(fwdt[...], window)
-                a, b = spectrum[:, :128], spectrum[:, 128:]
-                y = jnp.concatenate(
-                    [factor_real * a - factor_imaginary * b, factor_real * b + factor_imaginary * a], 1
-                ).astype(BF)
-                line = dot(invt[...], y).astype(BF)
-                out_a[0, n * BLOCK : (n + 1) * BLOCK, :] = line[:, :128]
-                out_a[1, n * BLOCK : (n + 1) * BLOCK, :] = line[:, 128:]
-        else:
-            phase = travel_phase(trav[1], iota((1, 256), 1) & 127)
-            factor_real = jnp.cos(phase)
-            factor_imaginary = jnp.sin(phase)
-            for part in range(2):
-                extt[part, :, 0 : tile_rows + 2 * MARGIN] = dot_nt(anti, ext[1, part]).astype(BF)
-                extt[part, :, tile_rows + 2 * MARGIN :] = jnp.zeros((BLOCK, MARGIN * 2), BF)
-            for n in range(quarters):
-                window = extt[:, :, n * BLOCK : (n + 2) * BLOCK].reshape(2 * BLOCK, 2 * BLOCK)
-                spectrum = dot(window[:, :WIN], fwd[...])
-                a, b = spectrum[:BLOCK], spectrum[BLOCK:]
-                y = jnp.concatenate(
-                    [factor_real * a - factor_imaginary * b, factor_real * b + factor_imaginary * a], 0
-                ).astype(BF)
-                line = dot(y, inv[...]).astype(BF)
-                out_b[0, :, n * BLOCK : (n + 1) * BLOCK] = line[:BLOCK]
-                out_b[1, :, n * BLOCK : (n + 1) * BLOCK] = line[BLOCK:]
+        finish(v, quarters - 1)
 
     left(0, vol.at[:, pl.ds(0, tile_rows - LINES), :])
     left(1, wa.at[:, pl.ds(0, tile_rows - LINES), :])
@@ -428,10 +463,24 @@
     tile_rows = nc * LINES
     quarters = tile_rows // BLOCK
     col_tiles, row_tiles = nc, nr * quarters
-    vmem = pl.BlockSpec(memory_space=pltpu.VMEM)
-    smem = pl.BlockSpec(memory_space=pltpu.SMEM)
+    anywhere = pl.BlockSpec(memory_space=pl.ANY)
     lines = (2, LINES, 128)
     scratch = [
+        pltpu.VMEM((2, tile_rows, 128), BF),
+        pltpu.VMEM((2, tile_rows, 128), BF),
+        pltpu.VMEM((2, BLOCK, tile_rows), BF),
+        pltpu.SMEM(sr.shape, jnp.int32),
+        pltpu.SMEM(sc.shape, jnp.int32),
+        pltpu.SMEM(trav.shape, F32),
+        pltpu.VMEM(sr.shape, jnp.int32),
+        pltpu.VMEM(fr.shape, F32),
+        pltpu.VMEM(sc.shape, jnp.int32),
+        pltpu.VMEM(fc.shape, F32),
+        pltpu.VMEM((WIN, 256), BF),
+        pltpu.VMEM((256, BLOCK), BF),
+        pltpu.VMEM((256, WIN), BF),
+        pltpu.VMEM((BLOCK, 256), BF),
+        pltpu.SemaphoreType.DMA((14,)),
         pltpu.VMEM((2, tile_rows, 128), BF),
         pltpu.VMEM((col_tiles, *lines), BF),
         pltpu.VMEM((col_tiles, *lines), BF),
@@ -449,30 +498,46 @@
         pltpu.VMEM((2, col_tiles + 2, *lines), BF),
         pltpu.VMEM((2, col_tiles, *lines), BF),
         pltpu.VMEM((2, 2, tile_rows + 2 * MARGIN, 128), BF),
-        pltpu.VMEM((2, BLOCK, tile_rows + BLOCK), BF),
         pltpu.VMEM((6, 3, LINES, 128), F32),
         pltpu.VMEM((7, 256, 256), BF),
         pltpu.SemaphoreType.DMA((17,)),
         pltpu.SemaphoreType.DMA((41,)),
     ]
-    return pl.pallas_call(
+    result = pl.pallas_call(
         functools.partial(kernel, nr, nc),
         out_shape=(
-            jax.ShapeDtypeStruct((2, tile_rows, 128), BF),
-            jax.ShapeDtypeStruct((2, 128, tile_rows), BF),
+            pltpu.VMEM((2, tile_rows, 128), BF),
+            pltpu.VMEM((2, 128, tile_rows), BF),
         ),
-        in_specs=[vmem] * 3 + [smem] * 3 + [vmem] * 8,
-        out_specs=(vmem, vmem),
+        in_specs=[pl.BlockSpec(memory_space=pltpu.HBM)] * 12,
+        out_specs=(pl.BlockSpec(memory_space=pltpu.VMEM),) * 2,
         scratch_shapes=scratch,
         compiler_params=pltpu.CompilerParams(
-            collective_id=0, has_side_effects=True, vmem_limit_bytes=56 * 2**20
+            collective_id=0, has_side_effects=True, vmem_limit_bytes=65994752
         ),
         name="rotate_travel",
     )(
-        vol, wa, wb, sr, sc, trav, sr, fr, sc, fc,
+        vol, wa, wb, sr, fr, sc, fc, trav,
         jnp.asarray(forward, BF), jnp.asarray(inverse, BF),
         jnp.asarray(forward.T, BF), jnp.asarray(inverse.T, BF),
     )
+    return pl.pallas_call(
+        hand_over,
+        out_shape=tuple(jax.ShapeDtypeStruct(x.shape, x.dtype) for x in result),
+        in_specs=[anywhere] * 2,
+        out_specs=(anywhere, anywhere),
+        scratch_shapes=[pltpu.SemaphoreType.DMA((2,))],
+        compiler_params=pltpu.CompilerParams(vmem_limit_bytes=2 * 2**20),
+        name="hand_over",
+    )(*result)
+
+
+def hand_over(a, b, out_a, out_b, sem):
+    given = [pltpu.make_async_copy(a, out_a, sem.at[0]), pltpu.make_async_copy(b, out_b, sem.at[1])]
+    for copy in given:
+        copy.start()
+    for copy in given:
+        copy.wait()
 
 
 def solution(mesh):

time: 81.5 us -> 75.8 us (0.930)
  Pallas kernels: 78.3 us -> 75.1 us
  local copies, waits for them, and re-layouts: 2.42 us -> 0 us
    pallas_call x1 -> x2, Pallas kernels: 78.3 us -> 75.1 us  [the longest x1 74.3 us: on_device(): pl.pallas_call(functools.partial(kernel, nr, nc), out_shape=(pltpu.VMEM((...]
    unnamed x4 -> x0, local copies, waits for them, and re-layouts: 2.42 us -> none
where the time goes in v2:
time: 75.8 us
  Pallas kernels  75.1 us (99%)
    pallas_call x1, Pallas kernels, on_device(): pl.pallas_call(functools.partial(kernel, nr, nc), out_shape=(pltpu.VMEM((...  74.3 us

profile of v2, /device:TPU:8, one launch (start us, length us, event | category | flops | bytes accessed | tf_op | source)
XLA Modules:
  0.0 75.8 jit_solution(6656029506072118881)
XLA Ops:
  0.6 74.3 %rotate_travel.1 = (bf16[2,512,128]{2,1,0:T(8,128)(2,1)S(1)}, bf16[2,128,512]{2,1,0:T(8,128)(2,1)S(1)}) custom-call(bf16[2,512,128]{2,1,0:T(8,128)(2,1)} %vol_in.1, bf16[2,512,128]{2,1,0:T(8,128)(2,1)} %wa_in.1, bf16[2,128,512]{2,1,0:T(8,128)(2,1)} %wb_in.1, s32[2,2,512]{2,1,0:T(2,128)} %sr_in.1, f32[2,2,512]{2,1,0:T(2,128)} %fr_in.1, s32[2,128]{1,0:T(2,128)} %sc_in.1, ...), custom_call_target="tpu_custom_call" | custom-call | tf_op jit(solution)/shard_map/rotate_travel/pallas_call | solution.py:506
  74.9 0.8 %hand_over.1 = (bf16[2,512,128]{2,1,0:T(8,128)(2,1)}, bf16[2,128,512]{2,1,0:T(8,128)(2,1)}) custom-call(bf16[2,512,128]{2,1,0:T(8,128)(2,1)S(1)} %get-tuple-element.4.a, bf16[2,128,512]{2,1,0:T(8,128)(2,1)S(1)} %get-tuple-element.5.b), custom_call_target="tpu_custom_call" | custom-call | tf_op jit(solution)/shard_map/hand_over/pallas_call | solution.py:524

commit v3 on v2

--- a/solution.py
+++ b/solution.py
@@ -252,6 +252,7 @@
             after(far)
 
     send_wave(0, True)
+    send_wave(1, True)
     for v in range(2):
         if v == 0:
             arrived(0, rows0.at[pl.ds(0, nc - 1)])
@@ -269,8 +270,9 @@
 
         wait(depth - 1 if own else depth)
 
-    def rows_to_columns(v):
-        for i, k in enumerate(order):
+    def rows_to_columns(v, which=(0, 1, 2, 3)):
+        for i in which:
+            k = order[i]
             spot = pl.ds(pl.multiple_of(k * BLOCK, BLOCK), BLOCK)
             landed(17 + 4 * v + k, tile1.at[v], i == 3)
             for part in range(2):
@@ -293,24 +295,25 @@
                 )
         turn2[v, :, :, sixteen(r), :] = o2[v, pl.ds(r * quarters, quarters)]
 
-    def columns_to_rows(v):
-        for i, k in enumerate(order):
+    def columns_to_rows(v, which=(0, 1, 2, 3)):
+        for i in which:
+            k = order[i]
             spot = pl.ds(pl.multiple_of(k * BLOCK, BLOCK), BLOCK)
             arrived(25 + 4 * v + k, turn2.at[v, 0, :, pl.ds(0, BLOCK - LINES), :])
             for part in range(2):
                 tile2[v, part, spot, :] = dot_nt(eye, turn2[v, k, part]).astype(BF)
             to_quarter(9 + v, 9 + v, lambda peer: tile2.at[v, :, sixteen(peer), :], rows2.at[v, c], k, i == 3)
-        rows2[v, c] = tile2[v, :, sixteen(c), :]
+        if which[-1] == 3:
+            rows2[v, c] = tile2[v, :, sixteen(c), :]
 
     wrow_b[nc - 1 - c] = wbt[:, sixteen(c), :]
-    rows_to_columns(0)
     send_wave(0, False)
     send_wave(1, False)
+    rows_to_columns(0)
     rows_to_columns(1)
     shear_columns(0)
+    shear_columns(1)
     columns_to_rows(0)
-    shear_columns(1)
-    send_wave(1, True)
     columns_to_rows(1)
 
     for v in range(2):
@@ -373,25 +376,31 @@
     phase = travel_phase(trav[1], iota((1, 256), 1) & 127)
     along_real, along_imaginary = jnp.cos(phase), jnp.sin(phase)
 
-    def finish(v, n):
-        rows = slice(n * BLOCK, n * BLOCK + WIN)
-        spot = slice(n * BLOCK, (n + 1) * BLOCK)
+    def finish(v, blocks):
+        count = len(blocks)
+        rows = [slice(n * BLOCK, n * BLOCK + WIN) for n in blocks]
+        spots = [slice(n * BLOCK, (n + 1) * BLOCK) for n in blocks]
         if v == 0:
-            window = jnp.concatenate([ext[0, part, rows, :] for part in range(2)], 1)
+            window = jnp.concatenate([ext[0, part, at, :] for part in range(2) for at in rows], 1)
             spectrum = dot(fwdt[...], window)
-            a, b = spectrum[:, :128], spectrum[:, 128:]
-            y = jnp.concatenate([down_real * a - down_imaginary * b, down_real * b + down_imaginary * a], 1)
+            a, b = spectrum[:, : count * 128], spectrum[:, count * 128 :]
+            real, imaginary = (jnp.concatenate([x] * count, 1) for x in (down_real, down_imaginary))
+            y = jnp.concatenate([real * a - imaginary * b, real * b + imaginary * a], 1)
             line = dot(invt[...], y.astype(BF)).astype(BF)
-            out_a[0, spot, :] = line[:, :128]
-            out_a[1, spot, :] = line[:, 128:]
+            for part in range(2):
+                for i, at in enumerate(spots):
+                    out_a[part, at, :] = line[:, (part * count + i) * 128 : (part * count + i + 1) * 128]
         else:
-            window = jnp.concatenate([dot_nt(anti, ext[1, part, rows, :]).astype(BF) for part in range(2)], 0)
+            window = jnp.concatenate(
+                [dot_nt(anti, ext[1, part, at, :]).astype(BF) for part in range(2) for at in rows], 0
+            )
             spectrum = dot(window, fwd[...])
-            a, b = spectrum[:BLOCK], spectrum[BLOCK:]
+            a, b = spectrum[: count * BLOCK], spectrum[count * BLOCK :]
             y = jnp.concatenate([along_real * a - along_imaginary * b, along_real * b + along_imaginary * a], 0)
             line = dot(y.astype(BF), inv[...]).astype(BF)
-            out_b[0, :, spot] = line[:BLOCK]
-            out_b[1, :, spot] = line[BLOCK:]
+            for part in range(2):
+                for i, at in enumerate(spots):
+                    out_b[part, :, at] = line[(part * count + i) * BLOCK : (part * count + i + 1) * BLOCK]
 
     for v in range(2):
         for k in (0, quarters - 1, *range(1, quarters - 1)):
@@ -424,20 +433,17 @@
                 def _(v=v):
                     ext[v, :, bottom, :] = jnp.zeros((2, MARGIN, 128), BF)
 
-        for n in range(1, quarters - 1):
-            finish(v, n)
+        finish(v, tuple(range(1, quarters - 1)))
 
         @pl.when(r > 0)
         def _(v=v):
             down(v).wait_recv()
 
-        finish(v, 0)
-
         @pl.when(r < nr - 1)
         def _(v=v):
             up(v).wait_recv()
 
-        finish(v, quarters - 1)
+        finish(v, (0, quarters - 1))
 
     left(0, vol.at[:, pl.ds(0, tile_rows - LINES), :])
     left(1, wa.at[:, pl.ds(0, tile_rows - LINES), :])

time: 75.8 us -> 73.8 us (0.974)
  Pallas kernels: 75.1 us -> 73 us
    pallas_call x1, Pallas kernels: 74.3 us -> 72.2 us  [on_device(): pl.pallas_call(functools.partial(kernel, nr, nc), out_shape=(pltpu.VMEM((...]
where the time goes in v3:
time: 73.8 us; the launch traced here: 73.7 us
  Pallas kernels  73 us (99%)
    pallas_call x1, Pallas kernels, on_device(): pl.pallas_call(functools.partial(kernel, nr, nc), out_shape=(pltpu.VMEM((...  72.2 us

profile of v3, /device:TPU:8, one launch (start us, length us, event | category | flops | bytes accessed | tf_op | source)
XLA Modules:
  0.0 73.7 jit_solution(5434732649352300711)
XLA Ops:
  0.6 72.2 %rotate_travel.1 = (bf16[2,512,128]{2,1,0:T(8,128)(2,1)S(1)}, bf16[2,128,512]{2,1,0:T(8,128)(2,1)S(1)}) custom-call(bf16[2,512,128]{2,1,0:T(8,128)(2,1)} %vol_in.1, bf16[2,512,128]{2,1,0:T(8,128)(2,1)} %wa_in.1, bf16[2,128,512]{2,1,0:T(8,128)(2,1)} %wb_in.1, s32[2,2,512]{2,1,0:T(2,128)} %sr_in.1, f32[2,2,512]{2,1,0:T(2,128)} %fr_in.1, s32[2,128]{1,0:T(2,128)} %sc_in.1, ...), custom_call_target="tpu_custom_call" | custom-call | tf_op jit(solution)/shard_map/rotate_travel/pallas_call | solution.py:512
  72.8 0.8 %hand_over.1 = (bf16[2,512,128]{2,1,0:T(8,128)(2,1)}, bf16[2,128,512]{2,1,0:T(8,128)(2,1)}) custom-call(bf16[2,512,128]{2,1,0:T(8,128)(2,1)S(1)} %get-tuple-element.4.a, bf16[2,128,512]{2,1,0:T(8,128)(2,1)S(1)} %get-tuple-element.5.b), custom_call_target="tpu_custom_call" | custom-call | tf_op jit(solution)/shard_map/hand_over/pallas_call | solution.py:530

commit v4 on v3

--- a/solution.py
+++ b/solution.py
@@ -89,16 +89,10 @@
 
     barrier = pltpu.get_barrier_semaphore()
 
-    def greet_col(i, _):
+    for i in sorted(range(1, nc), key=lambda i: min(i // 2 % (nc // 4), nc // 4 - i // 2 % (nc // 4)), reverse=True):
         pl.semaphore_signal(barrier, inc=1, device_id={"col": lax.rem(c + i, nc)}, device_id_type=MESH)
-        return 0
-
-    def greet_row(i, _):
+    for i in range(1, nr):
         pl.semaphore_signal(barrier, inc=1, device_id={"row": lax.rem(r + i, nr)}, device_id_type=MESH)
-        return 0
-
-    lax.fori_loop(1, nc, greet_col, 0)
-    lax.fori_loop(1, nr, greet_row, 0)
     loads = [
         pltpu.make_async_copy(src, dst, load.at[i])
         for i, (src, dst) in enumerate([
@@ -144,12 +138,16 @@
             if far or step:
                 ship(src, dst, phase, landing, "row", base + lax.rem(place + step, width))
 
-    def to_quarter(phase, landing, src, dst, quarter, own):
-        for step in range(1 if own else 0, depth):
-            peer = quarter * depth + lax.rem(lax.rem(c, depth) + depth - step, depth)
-            ship(src, dst, phase, landing, "col", peer)
+    def to_quarter(phase, landing, src, dst, quarter, order, own):
+        chips = depth // 2
+        for step in order:
+            stem = quarter * depth + 2 * lax.rem(zone_z + step, chips)
+            ship(src, dst, phase, landing, "col", stem + 1 - core)
+            if step or not own:
+                ship(src, dst, phase, landing, "col", stem + core)
 
     near = lax.div(c, depth)
+    strip = jnp.where(c < 2, 0, jnp.where(c >= nc - 2, 1, 2 + near))
     order = [(1 - lax.div(near, 2)) * 2 + (1 - lax.rem(near, 2)), (1 - lax.div(near, 2)) * 2 + lax.rem(near, 2),
              lax.div(near, 2) * 2 + (1 - lax.rem(near, 2)), near]
 
@@ -263,12 +261,12 @@
         shear(3 * v, row_base(v, 0), 3, rows0, col_tiles, o1.at[v], side_c, after)
         tile1[v, :, sixteen(c), :] = o1[v, c]
 
+    def collected(landing, part, number):
+        whole = part.at[:, pl.ds(0, number * LINES), :]
+        pltpu.make_async_copy(whole, whole, recv.at[landing]).wait()
+
     def landed(landing, part, own):
-        def wait(number):
-            whole = part.at[:, pl.ds(0, number * LINES), :]
-            pltpu.make_async_copy(whole, whole, recv.at[landing]).wait()
-
-        wait(depth - 1 if own else depth)
+        collected(landing, part, depth - 1 if own else depth)
 
     def rows_to_columns(v, which=(0, 1, 2, 3)):
         for i in which:
@@ -302,7 +300,7 @@
             arrived(25 + 4 * v + k, turn2.at[v, 0, :, pl.ds(0, BLOCK - LINES), :])
             for part in range(2):
                 tile2[v, part, spot, :] = dot_nt(eye, turn2[v, k, part]).astype(BF)
-            to_quarter(9 + v, 9 + v, lambda peer: tile2.at[v, :, sixteen(peer), :], rows2.at[v, c], k, i == 3)
+            to_quarter(9 + v, 9 + v, lambda peer: tile2.at[v, :, sixteen(peer), :], rows2.at[v, c], k, (2, 1, 3, 0) if i % 2 else (0, 1, 3, 2), i == 3)
         if which[-1] == 3:
             rows2[v, c] = tile2[v, :, sixteen(c), :]
 
@@ -349,9 +347,9 @@
             line = dot(y.reshape(span * 2 * LINES, 256).astype(BF), inv[...])
             half[v, pl.ds(m, span)] = line.reshape(span, 2, LINES, 128).astype(BF)
             if v == 0:
-                to_col(11, 33 + near, lambda peer: half.at[0, peer], ext.at[0, :, spot, :], far)
+                to_col(11, 33 + strip, lambda peer: half.at[0, peer], ext.at[0, :, spot, :], far)
             else:
-                to_col(12, 37 + near, lambda peer: half.at[1, nc - 1 - peer], ext.at[1, :, spot, :], far)
+                to_col(12, 39 + strip, lambda peer: half.at[1, nc - 1 - peer], ext.at[1, :, spot, :], far)
         ext[v, :, spot, :] = half[v, c if v == 0 else nc - 1 - c]
 
     top = pl.ds(0, MARGIN)
@@ -402,16 +400,17 @@
                 for i, at in enumerate(spots):
                     out_b[part, :, at] = line[(part * count + i) * BLOCK : (part * count + i + 1) * BLOCK]
 
+    counts = [2, 2, depth - 2] + [depth] * (quarters - 2) + [depth - 2]
     for v in range(2):
-        for k in (0, quarters - 1, *range(1, quarters - 1)):
-
-            @pl.when(near == k)
+        for k in range(quarters + 2):
+
+            @pl.when(strip == k)
             def _(v=v, k=k):
-                landed(33 + 4 * v + k, ext.at[v], True)
-
-            @pl.when(near != k)
+                collected(33 + 6 * v + k, ext.at[v], counts[k] - 1)
+
+            @pl.when(strip != k)
             def _(v=v, k=k):
-                landed(33 + 4 * v + k, ext.at[v], False)
+                collected(33 + 6 * v + k, ext.at[v], counts[k])
 
             if k == 0:
 
@@ -423,7 +422,7 @@
                 def _(v=v):
                     ext[v, :, top, :] = jnp.zeros((2, MARGIN, 128), BF)
 
-            if k == quarters - 1:
+            if k == 1:
 
                 @pl.when(r < nr - 1)
                 def _(v=v):
@@ -507,7 +506,7 @@
         pltpu.VMEM((6, 3, LINES, 128), F32),
         pltpu.VMEM((7, 256, 256), BF),
         pltpu.SemaphoreType.DMA((17,)),
-        pltpu.SemaphoreType.DMA((41,)),
+        pltpu.SemaphoreType.DMA((45,)),
     ]
     result = pl.pallas_call(
         functools.partial(kernel, nr, nc),

time: 73.8 us -> 73 us (0.989)
    pallas_call x1, Pallas kernels: 72.2 us -> 71.5 us  [on_device(): pl.pallas_call(functools.partial(kernel, nr, nc), out_shape=(pltpu.VMEM((...]
where the time goes in v4:
time: 73 us; the launch traced here: 72.9 us
  Pallas kernels  72.3 us (99%)
    pallas_call x1, Pallas kernels, on_device(): pl.pallas_call(functools.partial(kernel, nr, nc), out_shape=(pltpu.VMEM((...  71.5 us

profile of v4, /device:TPU:8, one launch (start us, length us, event | category | flops | bytes accessed | tf_op | source)
XLA Modules:
  0.0 72.9 jit_solution(1566824212577393512)
XLA Ops:
  0.6 71.5 %rotate_travel.1 = (bf16[2,512,128]{2,1,0:T(8,128)(2,1)S(1)}, bf16[2,128,512]{2,1,0:T(8,128)(2,1)S(1)}) custom-call(bf16[2,512,128]{2,1,0:T(8,128)(2,1)} %vol_in.1, bf16[2,512,128]{2,1,0:T(8,128)(2,1)} %wa_in.1, bf16[2,128,512]{2,1,0:T(8,128)(2,1)} %wb_in.1, s32[2,2,512]{2,1,0:T(2,128)} %sr_in.1, f32[2,2,512]{2,1,0:T(2,128)} %fr_in.1, s32[2,128]{1,0:T(2,128)} %sc_in.1, ...), custom_call_target="tpu_custom_call" | custom-call | tf_op jit(solution)/shard_map/rotate_travel/pallas_call | solution.py:511
  72.1 0.8 %hand_over.1 = (bf16[2,512,128]{2,1,0:T(8,128)(2,1)}, bf16[2,128,512]{2,1,0:T(8,128)(2,1)}) custom-call(bf16[2,512,128]{2,1,0:T(8,128)(2,1)S(1)} %get-tuple-element.4.a, bf16[2,128,512]{2,1,0:T(8,128)(2,1)S(1)} %get-tuple-element.5.b), custom_call_target="tpu_custom_call" | custom-call | tf_op jit(solution)/shard_map/hand_over/pallas_call | solution.py:529

commit v5 on v4

--- a/solution.py
+++ b/solution.py
@@ -275,7 +275,7 @@
             landed(17 + 4 * v + k, tile1.at[v], i == 3)
             for part in range(2):
                 turn1[v, k, part] = dot_nt(eye, tile1[v, part, spot, :]).astype(BF)
-            for far in (True, False):
+            for far in (False, True):
                 to_row(
                     5 + v, 5 + v, lambda peer: turn1.at[v, k, :, sixteen(peer), :], cols.at[v, r * quarters + k], far
                 )
@@ -286,7 +286,7 @@
 
         shear(3 * v + 1, col_base(v), 4, cols.at[v], row_tiles, o2.at[v], side_r, lambda far: None)
         for k in order:
-            for far in (True, False):
+            for far in (False, True):
                 to_row(
                     7 + v, 25 + 4 * v + k, lambda peer: o2.at[v, peer * quarters + k],
                     turn2.at[v, k, :, sixteen(r), :], far,
@@ -319,7 +319,7 @@
         arrived(9 + v, rows2.at[v, pl.ds(0, nc - 1)])
         shear(3 * v + 2, row_base(v, 1), 3, rows2.at[v], col_tiles, rot, side_c, lambda far: None)
         arrived(1 + v, wave.at[pl.ds(0, nc - 1)])
-        group = 4
+        group = 8
 
         def through(g, _, v=v, wave=wave):
             m = g * group

time: 73 us -> 73.7 us (level); the launches traced: 72.9 us -> 72.6 us
  no operation moved by 1% of the time
where the time goes in v5:
time: 73.7 us; the launch traced here: 72.6 us
  Pallas kernels  72 us (98%)
    pallas_call x1, Pallas kernels, on_device(): pl.pallas_call(functools.partial(kernel, nr, nc), out_shape=(pltpu.VMEM((...  71.2 us

profile of v5, /device:TPU:8, one launch (start us, length us, event | category | flops | bytes accessed | tf_op | source)
XLA Modules:
  0.0 72.6 jit_solution(12627558357026708212)
XLA Ops:
  0.6 71.2 %rotate_travel.1 = (bf16[2,512,128]{2,1,0:T(8,128)(2,1)S(1)}, bf16[2,128,512]{2,1,0:T(8,128)(2,1)S(1)}) custom-call(bf16[2,512,128]{2,1,0:T(8,128)(2,1)} %vol_in.1, bf16[2,512,128]{2,1,0:T(8,128)(2,1)} %wa_in.1, bf16[2,128,512]{2,1,0:T(8,128)(2,1)} %wb_in.1, s32[2,2,512]{2,1,0:T(2,128)} %sr_in.1, f32[2,2,512]{2,1,0:T(2,128)} %fr_in.1, s32[2,128]{1,0:T(2,128)} %sc_in.1, ...), custom_call_target="tpu_custom_call" | custom-call | tf_op jit(solution)/shard_map/rotate_travel/pallas_call | solution.py:511
  71.8 0.8 %hand_over.1 = (bf16[2,512,128]{2,1,0:T(8,128)(2,1)}, bf16[2,128,512]{2,1,0:T(8,128)(2,1)}) custom-call(bf16[2,512,128]{2,1,0:T(8,128)(2,1)S(1)} %get-tuple-element.4.a, bf16[2,128,512]{2,1,0:T(8,128)(2,1)S(1)} %get-tuple-element.5.b), custom_call_target="tpu_custom_call" | custom-call | tf_op jit(solution)/shard_map/hand_over/pallas_call | solution.py:529
